TPU v7x, 1024 devices: a whole 4x4x32 slice. The times are simulated.
1024 devices in a mesh: row: 16 (over x, z_hi), col: 64 (over y, z_lo, core).
Axes of the slice: x: 4, y: 4, z: 32 (z_hi: 4, z_lo: 8; z = z_hi * 8 + z_lo), core: 2. Of those that a mesh axis runs over, the one named last changes fastest.
Arguments:
- iterate: bfloat16 [4096, 6144], P(('row', 'col')), may hold values from -0.25 to 0.25
Outputs:
- update: bfloat16 [4096, 6144], P('row', 'col')
All inputs are finite; a program needn't handle non-finite values.
Results may differ from a plain program's by a relative error of at most 0.0084.
Values may be sent and summed in bfloat16 or wider, within the bound.
A program may use at most 32 MiB of HBM per device.

v0:
```python
import math

import jax
import jax.numpy as jnp
from jax import lax
from jax.sharding import PartitionSpec as P

M = 4096
D = 6144


linear_weight = 3.4445
cubic_weight = -4.775
quintic_weight = 2.0315
output_gain = 0.2


def gather_rows(block_rows):
    return lax.all_gather(block_rows, "row", axis=0, tiled=True)


def strided_order(panel_rows, row_devices, col_devices):
    total_rows, column_count = panel_rows.shape
    per_device = total_rows // (row_devices * col_devices)
    grouped = panel_rows.reshape(row_devices, col_devices, per_device, column_count)
    return jnp.transpose(grouped, (1, 0, 2, 3)).reshape(total_rows, column_count)


def row_product(left_rows, right_rows):
    return lax.dot_general(
        left_rows, right_rows, (((1,), (1,)), ((), ())), preferred_element_type=jnp.float32
    )


def shards(iterate):
    scaled_tile = lax.all_to_all(iterate, "col", split_axis=1, concat_axis=0, tiled=True)
    row_devices = lax.axis_size("row")
    col_devices = lax.axis_size("col")
    strided_rows = gather_rows(iterate)
    panel_rows = lax.all_gather(scaled_tile, "col", axis=1, tiled=True)
    gram_tile = row_product(panel_rows, strided_rows).astype(jnp.bfloat16)
    gram_wide = lax.all_gather(gram_tile, "col", axis=1, tiled=True)
    scaled_columns = strided_order(gather_rows(scaled_tile), row_devices, col_devices)
    image_tile = jnp.dot(gram_wide, scaled_columns, preferred_element_type=jnp.float32).astype(
        jnp.bfloat16
    )
    image_columns = strided_order(gather_rows(image_tile), row_devices, col_devices)
    second_term = jnp.dot(gram_wide, image_columns, preferred_element_type=jnp.float32)
    combined = (
        linear_weight * scaled_tile.astype(jnp.float32)
        + cubic_weight * image_tile.astype(jnp.float32)
        + quintic_weight * second_term
    )
    update_tile = (output_gain * math.sqrt(max(M, D)) * combined).astype(jnp.bfloat16)
    return update_tile


def solution(mesh):
    return jax.shard_map(
        shards,
        mesh=mesh,
        in_specs=(P(("row", "col"), None),),
        out_specs=P("row", "col"),
        check_vma=False,
    )
```

profile of v0, /device:TPU:1, one launch (start us, length us, event | category | flops | bytes accessed | tf_op | source)
XLA Modules:
  0.0 497.8 jit_solution(3305315725480618573)
XLA Ops:
  6.5 0.0 all-gather.4.cloned.1.call-start
  6.5 0.9 all_to_all.14
  7.5 0.1 copy.8
  7.5 30.3 %all_to_all.19 = bf16[4,64,96]{2,0,1:T(4,128)(2,1)S(1)} all-to-all(bf16[4,64,96]{2,0,1:T(4,128)(2,1)S(1)} %copy.8), channel_id=1, replica_groups=mesh['row'=16,'col'=64] {'col'}, dimensions={1} | all-to-all | bytes 98304 | tf_op jit(solution)/shard_map/all_to_all | solution.py:36
  37.8 0.7 copy.9
  38.5 0.0 all-gather.4.cloned.1.call-update
  38.5 0.0 all-gather.6.cloned.1.call-start
  38.6 115.6 %all-gather = bf16[16,4,6144]{2,1,0:T(4,128)(2,1)S(1)} all-gather(bf16[1,4,6144]{2,1,0:T(4,128)(2,1)} %bitcast.24), channel_id=1, replica_groups=mesh['row'=16,'col'=64] {'row'}, dimensions={0}, use_global_device_ids=true | all-gather | bytes 835584 | tf_op jit(solution)/shard_map/all_gather | solution.py:19
  154.2 0.2 reshape.20
  154.4 48.1 %all-gather.4.cloned.1.call-done = bf16[256,6144]{0,1:T(8,128)(2,1)} async-done(((bf16[256,96]{0,1:T(8,128)(2,1)}), bf16[256,6144]{0,1:T(8,128)(2,1)}) %all-gather.4.cloned.1.call-update) | async-done | bytes 3145744 | tf_op jit(solution)/shard_map/all_gather | solution.py:40
  202.5 3.1 convolution_convert_fusion.1
  205.6 0.0 all-gather.6.cloned.1.call-update
  205.6 110.2 %all_gather.18 = bf16[4096,96]{1,0:T(8,128)(2,1)S(1)} all-gather(bf16[256,96]{1,0:T(8,128)(2,1)S(1)} %bitcast.23), channel_id=1, replica_groups=mesh['row'=16,'col'=64] {'row'}, dimensions={0}, use_global_device_ids=true | all-gather | bytes 835584 | tf_op jit(solution)/shard_map/all_gather | solution.py:19
  315.8 0.6 copy.11
  316.4 59.2 %all-gather.6.cloned.1.call-done = bf16[256,4096]{0,1:T(8,128)(2,1)} async-done(((bf16[256,64]{0,1:T(8,128)(2,1)}), bf16[256,4096]{0,1:T(8,128)(2,1)}) %all-gather.6.cloned.1.call-update) | async-done | bytes 2097168 | tf_op jit(solution)/shard_map/all_gather | solution.py:42
  375.6 2.1 convolution_convert_fusion
  377.7 109.8 %all_gather.19 = bf16[4096,96]{0,1:T(8,128)(2,1)S(1)} all-gather(bf16[256,96]{0,1:T(8,128)(2,1)S(1)} %convolution_convert_fusion), channel_id=1, replica_groups=mesh['row'=16,'col'=64] {'row'}, dimensions={0}, use_global_device_ids=true | all-gather | bytes 835584 | tf_op jit(solution)/shard_map/all_gather | solution.py:19
  487.5 0.0 copy-start
  487.5 0.6 copy.12
  488.2 0.0 copy-start.1
  488.2 0.6 copy.13
  488.7 0.0 copy-done
  488.8 1.0 copy-done.1
  489.8 1.2 fusion.2
Async XLA Ops:
  6.5 195.9 %all-gather.4.cloned.1.call-start = ((), (), s32[]{:S(2)}) async-start(), calls=%async_computation.1 | async-start | bytes 3194880 | tf_op jit(solution)/shard_map/all_gather | solution.py:40
  38.5 337.0 %all-gather.6.cloned.1.call-start = ((), (), s32[]{:S(2)}) async-start(), calls=%async_computation.2 | async-start | bytes 2129920 | tf_op jit(solution)/shard_map/all_gather | solution.py:42
  487.5 1.2 copy-start
  488.2 1.6 copy-start.1
Sparse Core Ops, SparseCore 0:
  38.6 163.7 all-gather.3
  205.7 169.7 all-gather.5
where the time goes:
time: 507 us; the launch traced here: 498 us
  blocking collectives  366 us (72%)
  waiting for transfers between devices  107 us (21%)
  between operations  13.5 us (3%)
  matrix products  6.43 us (1%)
    all_gather x3, blocking collectives, gather_rows(): return lax.all_gather(block_rows, 'row', axis=0, tiled=True)  336 us
    all_gather x1, waiting for transfers between devices, shards(): gram_wide = lax.all_gather(gram_tile, 'col', axis=1, tiled=True)  59.2 us
    all_gather x1, waiting for transfers between devices, shards(): panel_rows = lax.all_gather(scaled_tile, 'col', axis=1, tiled=True)  48.1 us
    all_to_all x1, blocking collectives, shards(): lax.all_to_all(iterate, 'col', split_axis=1, concat_axis=0, tiled=True)  30.3 us
  transfers between devices with their start and end apart: 2, of which 2 were waited for; matrix products, arithmetic and copies ran while one was open for 0% of the time, Pallas kernels for 0%

commit v1 on v0

v1 whole, which is shorter than its diff:
```python
import functools
import math

import jax
import jax.numpy as jnp
from jax import lax
from jax.experimental import pallas as pl
from jax.experimental.pallas import tpu as pltpu
from jax.sharding import PartitionSpec as P

M = 4096
D = 6144

linear_weight = 3.4445
cubic_weight = -4.775
quintic_weight = 2.0315
output_gain = 0.2

MESH = pl.DeviceIdType.MESH
ROWS = 64
WIDE = 384
STEPS = 16
PEERS = [(dx, dy) for dx in range(4) for dy in range(4)][1:]


def nt_dot(left, right):
    return lax.dot_general(
        left, right, (((1,), (1,)), ((), ())), preferred_element_type=jnp.float32
    )


def nn_dot(left, right):
    return jnp.dot(left, right, preferred_element_type=jnp.float32)


def await_bytes(ref, sem):
    pltpu.make_async_copy(ref, ref, sem).wait()


def kernel(
    x_ref,
    out_ref,
    pieces,
    tile32,
    xg,
    part,
    sums_in,
    wide,
    total,
    blocks,
    first_sem,
    ring_send,
    ring_recv,
    twin_send,
    twin_recv,
    rs_send,
    rs_recv,
    ag_send,
    ag_recv,
    last_send,
    last_recv,
):
    row = lax.axis_index("row")
    col = lax.axis_index("col")
    x, z_hi = row // 4, lax.rem(row, 4)
    y, z_lo, core = col // 16, lax.rem(col // 2, 8), lax.rem(col, 2)
    z = z_hi * 8 + z_lo

    def device(x_at, y_at, z_at, core_at):
        return (x_at * 4 + z_at // 8, y_at * 16 + lax.rem(z_at, 8) * 2 + core_at)

    def peer(dx, dy):
        return lax.rem(x + dx, 4), lax.rem(y + dy, 4)

    up = device(x, y, lax.rem(z + 1, 32), core)
    down = device(x, y, lax.rem(z + 31, 32), core)
    twin = (row, col + 1 - 2 * core)

    sends = []

    def push(src, dst, send_sem, recv_sem, target):
        copy = pltpu.make_async_remote_copy(
            src_ref=src,
            dst_ref=dst,
            send_sem=send_sem,
            recv_sem=recv_sem,
            device_id=target,
            device_id_type=MESH,
        )
        copy.start()
        return copy

    barrier = pltpu.get_barrier_semaphore()
    for dx, dy in PEERS:
        px, py = peer(dx, dy)
        pl.semaphore_signal(barrier, inc=1, device_id=device(px, py, z, core), device_id_type=MESH)
    for target in (up, down, twin):
        pl.semaphore_signal(barrier, inc=1, device_id=target, device_id_type=MESH)
    pl.semaphore_wait(barrier, 18)

    me = 4 * x + y
    for dx, dy in PEERS:
        px, py = peer(dx, dy)
        push(
            x_ref.at[4 * py + px],
            pieces.at[me],
            first_sem.at[0],
            first_sem.at[1],
            device(px, py, z, core),
        )
    pieces[me] = x_ref[4 * y + x]
    await_bytes(pieces.at[pl.ds(0, 15)], first_sem.at[1])
    for k in range(16):
        tile32[4 * k : 4 * k + 4, :] = pieces[k].astype(jnp.float32)
    last = 256 * 15
    xg[last : last + ROWS, :] = tile32[...].astype(jnp.bfloat16)
    await_bytes(pieces.at[pl.ds(0, 15)], first_sem.at[0])

    def slot(step, sign, mine):
        if step == 0:
            start = last
        elif step == STEPS:
            start = last + ROWS
        else:
            start = 256 * (step - 1) + (0 if sign > 0 else ROWS)
        return xg.at[pl.ds(start + (0 if mine else 2 * ROWS), ROWS), :]

    def sem_at(step, sign):
        return step if sign > 0 else STEPS + step

    def hop(step, sign):
        at = sem_at(step, sign)
        sends.append(
            push(
                slot(step - 1, sign, True),
                slot(step, sign, True),
                ring_send.at[at],
                ring_recv.at[at],
                up if sign > 0 else down,
            )
        )

    def share(step, sign):
        at = sem_at(step, sign)
        sends.append(
            push(
                slot(step, sign, True),
                slot(step, sign, False),
                twin_send.at[at],
                twin_recv.at[at],
                twin,
            )
        )

    tile = xg.at[pl.ds(last, ROWS), :]

    def partial(stage, left, group):
        b, g = group // 4, group % 4
        part[stage, b, :, 256 * g : 256 * g + 256] = nt_dot(
            left, xg[256 * group : 256 * group + 256, :]
        ).astype(jnp.bfloat16)

    def scatter(stage, b):
        for k, (dx, dy) in enumerate(PEERS):
            px, py = peer(dx, dy)
            push(
                part.at[
                    stage,
                    b,
                    pl.ds(pl.multiple_of(16 * px, 16), 16),
                    pl.ds(pl.multiple_of(256 * py, 256), 256),
                ],
                sums_in.at[stage, b, k],
                rs_send.at[stage, b],
                rs_recv.at[stage, b],
                device(px, py, z, core),
            )

    def spread(stage, b):
        await_bytes(sums_in.at[stage, b], rs_recv.at[stage, b])
        rows = pl.ds(pl.multiple_of(16 * x, 16), 16)
        columns = pl.ds(pl.multiple_of(256 * y, 256), 256)
        acc = part[stage, b, rows, columns].astype(jnp.float32)
        for k in range(15):
            acc += sums_in[stage, b, k].astype(jnp.float32)
        wide[stage, b, rows, columns] = acc.astype(jnp.bfloat16)
        for dx, dy in PEERS:
            px, py = peer(dx, dy)
            push(
                wide.at[stage, b, rows, columns],
                wide.at[stage, b, rows, columns],
                ag_send.at[stage, b],
                ag_recv.at[stage, b],
                device(px, py, z, core),
            )

    def accumulate(stage, b):
        await_bytes(sums_in.at[stage, b], ag_recv.at[stage, b])
        product = nn_dot(wide[stage, b], xg[1024 * b : 1024 * b + 1024, :])
        if b == 0:
            total[stage] = product
        else:
            total[stage] += product

    share(0, 1)
    hop(1, 1)
    hop(1, -1)

    def ready(step):
        for sign in (1, -1):
            if step == STEPS and sign < 0:
                continue
            at = sem_at(step, sign)
            await_bytes(slot(step, sign, False), twin_recv.at[at])

    todo = {
        5: lambda: scatter(0, 0),
        9: lambda: (spread(0, 0), scatter(0, 1)),
        13: lambda: (accumulate(0, 0), spread(0, 1), scatter(0, 2)),
        16: lambda: (accumulate(0, 1),),
    }
    for step in range(1, STEPS + 1):
        for sign in (1, -1):
            if step == STEPS and sign < 0:
                continue
            await_bytes(slot(step, sign, True), ring_recv.at[sem_at(step, sign)])
            if step < STEPS and not (step == STEPS - 1 and sign < 0):
                hop(step + 1, sign)
        for sign in (1, -1):
            if not (step == STEPS and sign < 0):
                share(step, sign)
        if step > 1:
            ready(step - 1)
            partial(0, tile[...], step - 2)
        if step in todo:
            todo[step]()
    await_bytes(slot(0, 1, False), twin_recv.at[0])
    ready(STEPS)
    partial(0, tile[...], 15)
    scatter(0, 3)
    spread(0, 2)
    accumulate(0, 2)
    spread(0, 3)
    accumulate(0, 3)

    image = total[0].astype(jnp.bfloat16)
    for b in range(4):
        for g in range(4):
            partial(1, image, 4 * b + g)
        scatter(1, b)
    for b in range(4):
        spread(1, b)
    for b in range(4):
        accumulate(1, b)

    update = (output_gain * math.sqrt(max(M, D))) * (
        linear_weight * tile[...].astype(jnp.float32)
        + cubic_weight * image.astype(jnp.float32)
        + quintic_weight * total[1]
    )
    update = jnp.concatenate([update, jnp.zeros((ROWS, 128), jnp.float32)], axis=1)
    for j in range(4):
        block = update[:, 96 * j : 96 * j + 128].astype(jnp.bfloat16)
        for k in range(4):
            blocks[k, j] = block[16 * k : 16 * k + 16, :]

    landing = z_lo * 2 + core
    first_col = 16 * y + 4 * x

    def last_copy(k, j):
        return pltpu.make_async_remote_copy(
            src_ref=blocks.at[k, j],
            dst_ref=out_ref.at[landing],
            send_sem=last_send.at[4 * k + j],
            recv_sem=last_recv.at[landing],
            device_id=(4 * k + z_hi, first_col + j),
            device_id_type=MESH,
        )

    for k in range(4):
        for j in range(4):
            away = jnp.logical_or(x != k, col != first_col + j)

            @pl.when(away)
            def _(k=k, j=j):
                last_copy(k, j).start()

            @pl.when(jnp.logical_not(away))
            def _(k=k, j=j):
                pltpu.make_async_copy(
                    blocks.at[k, j], out_ref.at[landing], last_recv.at[landing]
                ).start()

    for copy in sends:
        copy.wait_send()
    for stage in range(2):
        for b in range(4):
            await_bytes(sums_in.at[stage, b], rs_send.at[stage, b])
            await_bytes(sums_in.at[stage, b], ag_send.at[stage, b])
    for k in range(16):
        await_bytes(out_ref.at[k], last_recv.at[k])
    for k in range(4):
        for j in range(4):

            @pl.when(jnp.logical_or(x != k, col != first_col + j))
            def _(k=k, j=j):
                last_copy(k, j).wait_send()


def shards(iterate):
    pieces = jnp.transpose(iterate.reshape(4, 16, WIDE), (1, 0, 2))
    spec = pl.BlockSpec(memory_space=pltpu.VMEM)
    landed = pl.pallas_call(
        kernel,
        out_shape=jax.ShapeDtypeStruct((16, 16, 128), jnp.bfloat16),
        in_specs=[spec],
        out_specs=spec,
        scratch_shapes=[
            pltpu.VMEM((16, 4, WIDE), jnp.bfloat16),
            pltpu.VMEM((ROWS, WIDE), jnp.float32),
            pltpu.VMEM((M, WIDE), jnp.bfloat16),
            pltpu.VMEM((2, 4, ROWS, 1024), jnp.bfloat16),
            pltpu.VMEM((2, 4, 15, 16, 256), jnp.bfloat16),
            pltpu.VMEM((2, 4, ROWS, 1024), jnp.bfloat16),
            pltpu.VMEM((2, ROWS, WIDE), jnp.float32),
            pltpu.VMEM((4, 4, 16, 128), jnp.bfloat16),
            pltpu.SemaphoreType.DMA((2,)),
            pltpu.SemaphoreType.DMA((32,)),
            pltpu.SemaphoreType.DMA((32,)),
            pltpu.SemaphoreType.DMA((32,)),
            pltpu.SemaphoreType.DMA((32,)),
            pltpu.SemaphoreType.DMA((2, 4)),
            pltpu.SemaphoreType.DMA((2, 4)),
            pltpu.SemaphoreType.DMA((2, 4)),
            pltpu.SemaphoreType.DMA((2, 4)),
            pltpu.SemaphoreType.DMA((16,)),
            pltpu.SemaphoreType.DMA((16,)),
        ],
        compiler_params=pltpu.CompilerParams(collective_id=0, has_side_effects=True),
    )(pieces)
    tiles = landed.reshape(16, 4, 4, 128)[..., :96]
    return jnp.transpose(tiles, (1, 0, 2, 3)).reshape(256, 96)


def solution(mesh):
    return jax.shard_map(
        shards,
        mesh=mesh,
        in_specs=(P(("row", "col"), None),),
        out_specs=P("row", "col"),
        check_vma=False,
    )
```

time: 507 us -> 123 us (0.24); the launches traced: 498 us -> 122 us
  blocking collectives: 366 us -> 0 us
  Pallas kernels: 0 us -> 121 us
  waiting for transfers between devices: 107 us -> 0 us
  between operations: 13.5 us -> 0.01 us
  matrix products: 6.43 us -> 0 us
    all_gather x3 -> x0, blocking collectives: 336 us -> none  [gather_rows(): return lax.all_gather(block_rows, 'row', axis=0, tiled=True)]
    pallas_call x0 -> x1, Pallas kernels: none -> 121 us  [shards(): pl.pallas_call(kernel, out_shape=jax.ShapeDtypeStruct((16, 16, 128), jnp....]
    all_gather x2 -> x0, waiting for transfers between devices: 107 us -> none  [the longest x1 59.2 us: shards(): gram_wide = lax.all_gather(gram_tile, 'col', axis=1, tiled=True)]
    all_to_all x1 -> x0, blocking collectives: 30.3 us -> none  [shards(): lax.all_to_all(iterate, 'col', split_axis=1, concat_axis=0, tiled=True)]
    dot_general x3 -> x0, matrix products: 6.43 us -> none  [the longest x1 3.12 us: row_product(): lax.dot_general(left_rows, right_rows, (((1,), (1,)), ((), ())), preferre...]
  transfers between devices with their start and end apart: 2 -> 0, of which waited for: 2 -> 0; matrix products, arithmetic and copies ran while one was open for 0% -> 0% of each run, Pallas kernels for 0% -> 0%
where the time goes in v1:
time: 123 us; the launch traced here: 122 us
  Pallas kernels  121 us (98%)
  local copies, waits for them, and re-layouts  1.59 us (1%)
    pallas_call x1, Pallas kernels, shards(): pl.pallas_call(kernel, out_shape=jax.ShapeDtypeStruct((16, 16, 128), jnp....  121 us

profile of v1, /device:TPU:1, one launch (start us, length us, event | category | flops | bytes accessed | tf_op | source)
XLA Modules:
  0.0 122.4 jit_solution(1536377944418219774)
XLA Ops:
  0.0 120.8 %shard_map.17 = bf16[16,16,128]{2,1,0:T(8,128)(2,1)} custom-call(bf16[16,4,384]{2,1,0:T(4,128)(2,1)} %bitcast.10), custom_call_target="tpu_custom_call" | custom-call | tf_op jit(solution)/shard_map/pallas_call | solution.py:313
  120.8 0.9 copy.5
  121.6 0.7 copy.4

commit v2 on v1

--- a/solution.py
+++ b/solution.py
@@ -20,7 +20,35 @@
 ROWS = 64
 WIDE = 384
 STEPS = 16
-PEERS = [(dx, dy) for dx in range(4) for dy in range(4)][1:]
+STRIDE = 3
+
+
+def taken_from():
+    source = {}
+    for far in range(1, STEPS + 1):
+        stop = (2 * far + STRIDE) // (2 * STRIDE) * STRIDE
+        stop -= STRIDE if stop >= STEPS else 0
+        source[far] = far - STRIDE if far == stop else far - 1 if far > stop else far + 1
+    return source
+
+
+SOURCE = taken_from()
+CHILDREN = {
+    far: sorted((c for c in SOURCE if SOURCE[c] == far), key=lambda c: -abs(c - far))
+    for far in range(STEPS + 1)
+}
+
+
+def arrival(far):
+    return 0.0 if far == 0 else arrival(SOURCE[far]) + 3.3 + 0.8 * abs(far - SOURCE[far])
+
+
+ORDER = sorted(range(1, STEPS + 1), key=lambda far: (arrival(far), far))
+REACH = sorted({s * (c - SOURCE[c]) for c in SOURCE for s in (1, -1)})
+PEERS = sorted(
+    [(dx, dy) for dx in range(4) for dy in range(4)][1:],
+    key=lambda d: -min(d[0], 4 - d[0]) - min(d[1], 4 - d[1]),
+)
 
 
 def nt_dot(left, right):
@@ -48,6 +76,8 @@
     wide,
     total,
     blocks,
+    landed,
+    out32,
     first_sem,
     ring_send,
     ring_recv,
@@ -72,9 +102,10 @@
     def peer(dx, dy):
         return lax.rem(x + dx, 4), lax.rem(y + dy, 4)
 
-    up = device(x, y, lax.rem(z + 1, 32), core)
-    down = device(x, y, lax.rem(z + 31, 32), core)
-    twin = (row, col + 1 - 2 * core)
+    def column(far):
+        return lax.rem(z + 32 + far, 32)
+
+    twin = device(x, y, z, 1 - core)
 
     sends = []
 
@@ -94,9 +125,11 @@
     for dx, dy in PEERS:
         px, py = peer(dx, dy)
         pl.semaphore_signal(barrier, inc=1, device_id=device(px, py, z, core), device_id_type=MESH)
-    for target in (up, down, twin):
-        pl.semaphore_signal(barrier, inc=1, device_id=target, device_id_type=MESH)
-    pl.semaphore_wait(barrier, 18)
+    greeted = [(x, y, column(far), core) for far in REACH]
+    greeted.append((x, y, z, 1 - core))
+    for target in greeted:
+        pl.semaphore_signal(barrier, inc=1, device_id=device(*target), device_id_type=MESH)
+    pl.semaphore_wait(barrier, 15 + len(greeted))
 
     me = 4 * x + y
     for dx, dy in PEERS:
@@ -114,43 +147,55 @@
         tile32[4 * k : 4 * k + 4, :] = pieces[k].astype(jnp.float32)
     last = 256 * 15
     xg[last : last + ROWS, :] = tile32[...].astype(jnp.bfloat16)
-    await_bytes(pieces.at[pl.ds(0, 15)], first_sem.at[0])
-
-    def slot(step, sign, mine):
-        if step == 0:
+
+    def slot(far, sign, mine):
+        if far == 0:
             start = last
-        elif step == STEPS:
+        elif far == STEPS:
             start = last + ROWS
         else:
-            start = 256 * (step - 1) + (0 if sign > 0 else ROWS)
+            start = 256 * ORDER.index(far) + (0 if sign > 0 else ROWS)
         return xg.at[pl.ds(start + (0 if mine else 2 * ROWS), ROWS), :]
 
-    def sem_at(step, sign):
-        return step if sign > 0 else STEPS + step
-
-    def hop(step, sign):
-        at = sem_at(step, sign)
-        sends.append(
-            push(
-                slot(step - 1, sign, True),
-                slot(step, sign, True),
-                ring_send.at[at],
-                ring_recv.at[at],
-                up if sign > 0 else down,
+    def sem_at(far, sign):
+        return far if sign > 0 else STEPS + far
+
+    def signs(far):
+        return (1,) if far in (0, STEPS) else (1, -1)
+
+    def hand_on(far):
+        for child in CHILDREN[far]:
+            for sign in (1, -1):
+                if child == STEPS and sign < 0:
+                    continue
+                at = sem_at(child, sign)
+                target = column(sign * (child - far))
+                sends.append(
+                    push(
+                        slot(far, sign, True),
+                        slot(child, sign, True),
+                        ring_send.at[at],
+                        ring_recv.at[at],
+                        device(x, y, target, core),
+                    )
+                )
+
+    def share(far):
+        for sign in signs(far):
+            at = sem_at(far, sign)
+            sends.append(
+                push(
+                    slot(far, sign, True),
+                    slot(far, sign, False),
+                    twin_send.at[at],
+                    twin_recv.at[at],
+                    twin,
+                )
             )
-        )
-
-    def share(step, sign):
-        at = sem_at(step, sign)
-        sends.append(
-            push(
-                slot(step, sign, True),
-                slot(step, sign, False),
-                twin_send.at[at],
-                twin_recv.at[at],
-                twin,
-            )
-        )
+
+    def shared(far):
+        for sign in signs(far):
+            await_bytes(slot(far, sign, False), twin_recv.at[sem_at(far, sign)])
 
     tile = xg.at[pl.ds(last, ROWS), :]
 
@@ -202,45 +247,45 @@
         else:
             total[stage] += product
 
-    share(0, 1)
-    hop(1, 1)
-    hop(1, -1)
-
-    def ready(step):
-        for sign in (1, -1):
-            if step == STEPS and sign < 0:
-                continue
-            at = sem_at(step, sign)
-            await_bytes(slot(step, sign, False), twin_recv.at[at])
-
-    todo = {
-        5: lambda: scatter(0, 0),
-        9: lambda: (spread(0, 0), scatter(0, 1)),
-        13: lambda: (accumulate(0, 0), spread(0, 1), scatter(0, 2)),
-        16: lambda: (accumulate(0, 1),),
-    }
-    for step in range(1, STEPS + 1):
-        for sign in (1, -1):
-            if step == STEPS and sign < 0:
-                continue
-            await_bytes(slot(step, sign, True), ring_recv.at[sem_at(step, sign)])
-            if step < STEPS and not (step == STEPS - 1 and sign < 0):
-                hop(step + 1, sign)
-        for sign in (1, -1):
-            if not (step == STEPS and sign < 0):
-                share(step, sign)
-        if step > 1:
-            ready(step - 1)
-            partial(0, tile[...], step - 2)
-        if step in todo:
-            todo[step]()
-    await_bytes(slot(0, 1, False), twin_recv.at[0])
-    ready(STEPS)
-    partial(0, tile[...], 15)
-    scatter(0, 3)
-    spread(0, 2)
-    accumulate(0, 2)
+    hand_on(0)
+    share(0)
+    groups, spreads, sums = list(range(15)), [], []
+    for far in ORDER:
+        now = arrival(far)
+        for sign in signs(far):
+            await_bytes(slot(far, sign, True), ring_recv.at[sem_at(far, sign)])
+        hand_on(far)
+        share(far)
+        while groups and arrival(ORDER[groups[0]]) + 4.0 <= now:
+            group = groups.pop(0)
+            shared(ORDER[group])
+            partial(0, tile[...], group)
+            if group % 4 == 3:
+                scatter(0, group // 4)
+                spreads.append((now + 8.0, group // 4))
+        while spreads and spreads[0][0] <= now:
+            b = spreads.pop(0)[1]
+            spread(0, b)
+            sums.append((now + 8.0, b))
+        while sums and sums[0][0] <= now:
+            accumulate(0, sums.pop(0)[1])
+    for group in groups + [15]:
+        if group < 15:
+            shared(ORDER[group])
+        else:
+            shared(STEPS)
+            shared(0)
+        partial(0, tile[...], group)
+        if group % 4 == 3:
+            scatter(0, group // 4)
+            spreads.append((0.0, group // 4))
+    for _, b in spreads[:-1]:
+        spread(0, b)
+        sums.append((0.0, b))
+    for _, b in sums[:-1]:
+        accumulate(0, b)
     spread(0, 3)
+    accumulate(0, sums[-1][1])
     accumulate(0, 3)
 
     image = total[0].astype(jnp.bfloat16)
@@ -270,7 +315,7 @@
     def last_copy(k, j):
         return pltpu.make_async_remote_copy(
             src_ref=blocks.at[k, j],
-            dst_ref=out_ref.at[landing],
+            dst_ref=landed.at[landing],
             send_sem=last_send.at[4 * k + j],
             recv_sem=last_recv.at[landing],
             device_id=(4 * k + z_hi, first_col + j),
@@ -288,17 +333,22 @@
             @pl.when(jnp.logical_not(away))
             def _(k=k, j=j):
                 pltpu.make_async_copy(
-                    blocks.at[k, j], out_ref.at[landing], last_recv.at[landing]
+                    blocks.at[k, j], landed.at[landing], last_recv.at[landing]
                 ).start()
 
+    for k in range(16):
+        await_bytes(landed.at[k], last_recv.at[k])
+        block = landed[k].astype(jnp.float32)
+        for j in range(4):
+            out32[64 * j + 4 * k : 64 * j + 4 * k + 4, :] = block[4 * j : 4 * j + 4, :]
+    out_ref[...] = out32[:, :96].astype(jnp.bfloat16)
+    await_bytes(pieces.at[pl.ds(0, 15)], first_sem.at[0])
     for copy in sends:
         copy.wait_send()
     for stage in range(2):
         for b in range(4):
             await_bytes(sums_in.at[stage, b], rs_send.at[stage, b])
             await_bytes(sums_in.at[stage, b], ag_send.at[stage, b])
-    for k in range(16):
-        await_bytes(out_ref.at[k], last_recv.at[k])
     for k in range(4):
         for j in range(4):
 
@@ -310,9 +360,9 @@
 def shards(iterate):
     pieces = jnp.transpose(iterate.reshape(4, 16, WIDE), (1, 0, 2))
     spec = pl.BlockSpec(memory_space=pltpu.VMEM)
-    landed = pl.pallas_call(
+    return pl.pallas_call(
         kernel,
-        out_shape=jax.ShapeDtypeStruct((16, 16, 128), jnp.bfloat16),
+        out_shape=jax.ShapeDtypeStruct((256, 96), jnp.bfloat16),
         in_specs=[spec],
         out_specs=spec,
         scratch_shapes=[
@@ -324,6 +374,8 @@
             pltpu.VMEM((2, 4, ROWS, 1024), jnp.bfloat16),
             pltpu.VMEM((2, ROWS, WIDE), jnp.float32),
             pltpu.VMEM((4, 4, 16, 128), jnp.bfloat16),
+            pltpu.VMEM((16, 16, 128), jnp.bfloat16),
+            pltpu.VMEM((256, 128), jnp.float32),
             pltpu.SemaphoreType.DMA((2,)),
             pltpu.SemaphoreType.DMA((32,)),
             pltpu.SemaphoreType.DMA((32,)),
@@ -338,8 +390,6 @@
         ],
         compiler_params=pltpu.CompilerParams(collective_id=0, has_side_effects=True),
     )(pieces)
-    tiles = landed.reshape(16, 4, 4, 128)[..., :96]
-    return jnp.transpose(tiles, (1, 0, 2, 3)).reshape(256, 96)
 
 
 def solution(mesh):

time: 123 us -> 104 us (0.85)
  Pallas kernels: 121 us -> 101 us
    pallas_call x1, Pallas kernels: 121 us -> 101 us  [shards(): pl.pallas_call(kernel, out_shape=jax.ShapeDtypeStruct((256, 96), jnp.bflo...]
    pallas_call x0 -> x1, local copies, waits for them, and re-layouts: none -> 1.56 us  [shards(): pl.pallas_call(kernel, out_shape=jax.ShapeDtypeStruct((256, 96), jnp.bflo...]
where the time goes in v2:
time: 104 us; the launch traced here: 102 us
  Pallas kernels  101 us (97%)
  local copies, waits for them, and re-layouts  1.56 us (2%)
    pallas_call x1, Pallas kernels, shards(): pl.pallas_call(kernel, out_shape=jax.ShapeDtypeStruct((256, 96), jnp.bflo...  101 us

profile of v2, /device:TPU:1, one launch (start us, length us, event | category | flops | bytes accessed | tf_op | source)
XLA Modules:
  0.0 102.4 jit_solution(14420173187588864300)
XLA Ops:
  0.0 100.8 %shard_map.17 = bf16[256,96]{1,0:T(8,128)(2,1)} custom-call(bf16[16,4,384]{2,1,0:T(4,128)(2,1)} %bitcast.3), custom_call_target="tpu_custom_call" | custom-call | tf_op jit(solution)/shard_map/pallas_call | solution.py:363
  100.9 1.6 %copy.2 = bf16[256,96]{0,1:T(8,128)(2,1)} copy(bf16[256,96]{1,0:T(8,128)(2,1)} %shard_map.17) | data formatting | bytes 98304 | tf_op jit(solution)/shard_map/pallas_call | solution.py:363

commit v3 on v2

--- a/solution.py
+++ b/solution.py
@@ -21,6 +21,8 @@
 WIDE = 384
 STEPS = 16
 STRIDE = 3
+PARTS = 2
+PIECE = ROWS // PARTS
 
 
 def taken_from():
@@ -40,7 +42,10 @@
 
 
 def arrival(far):
-    return 0.0 if far == 0 else arrival(SOURCE[far]) + 3.3 + 0.8 * abs(far - SOURCE[far])
+    if far == 0:
+        return 0.0
+    hops = abs(far - SOURCE[far])
+    return arrival(SOURCE[far]) + 3.3 + 0.8 * hops + (6.0 if hops == 1 else 0.0)
 
 
 ORDER = sorted(range(1, STEPS + 1), key=lambda far: (arrival(far), far))
@@ -148,14 +153,17 @@
     last = 256 * 15
     xg[last : last + ROWS, :] = tile32[...].astype(jnp.bfloat16)
 
-    def slot(far, sign, mine):
+    def slot(far, sign, mine, part_of=None):
         if far == 0:
             start = last
         elif far == STEPS:
             start = last + ROWS
         else:
             start = 256 * ORDER.index(far) + (0 if sign > 0 else ROWS)
-        return xg.at[pl.ds(start + (0 if mine else 2 * ROWS), ROWS), :]
+        start += 0 if mine else 2 * ROWS
+        if part_of is None:
+            return xg.at[pl.ds(start, ROWS), :]
+        return xg.at[pl.ds(start + PIECE * part_of, PIECE), :]
 
     def sem_at(far, sign):
         return far if sign > 0 else STEPS + far
@@ -163,20 +171,19 @@
     def signs(far):
         return (1,) if far in (0, STEPS) else (1, -1)
 
-    def hand_on(far):
+    def hand_on(far, which, piece):
         for child in CHILDREN[far]:
-            for sign in (1, -1):
+            for sign in which:
                 if child == STEPS and sign < 0:
                     continue
                 at = sem_at(child, sign)
-                target = column(sign * (child - far))
                 sends.append(
                     push(
-                        slot(far, sign, True),
-                        slot(child, sign, True),
-                        ring_send.at[at],
-                        ring_recv.at[at],
-                        device(x, y, target, core),
+                        slot(far, sign, True, piece),
+                        slot(child, sign, True, piece),
+                        ring_send.at[piece, at],
+                        ring_recv.at[piece, at],
+                        device(x, y, column(sign * (child - far)), core),
                     )
                 )
 
@@ -247,14 +254,16 @@
         else:
             total[stage] += product
 
-    hand_on(0)
+    for piece in range(PARTS):
+        hand_on(0, (1, -1), piece)
     share(0)
     groups, spreads, sums = list(range(15)), [], []
     for far in ORDER:
         now = arrival(far)
-        for sign in signs(far):
-            await_bytes(slot(far, sign, True), ring_recv.at[sem_at(far, sign)])
-        hand_on(far)
+        for piece in range(PARTS):
+            for sign in signs(far):
+                await_bytes(slot(far, sign, True, piece), ring_recv.at[piece, sem_at(far, sign)])
+                hand_on(far, (sign,), piece)
         share(far)
         while groups and arrival(ORDER[groups[0]]) + 4.0 <= now:
             group = groups.pop(0)
@@ -377,8 +386,8 @@
             pltpu.VMEM((16, 16, 128), jnp.bfloat16),
             pltpu.VMEM((256, 128), jnp.float32),
             pltpu.SemaphoreType.DMA((2,)),
-            pltpu.SemaphoreType.DMA((32,)),
-            pltpu.SemaphoreType.DMA((32,)),
+            pltpu.SemaphoreType.DMA((PARTS, 32)),
+            pltpu.SemaphoreType.DMA((PARTS, 32)),
             pltpu.SemaphoreType.DMA((32,)),
             pltpu.SemaphoreType.DMA((32,)),
             pltpu.SemaphoreType.DMA((2, 4)),

time: 104 us -> 98.2 us (0.944)
  Pallas kernels: 101 us -> 96.1 us
    pallas_call x1, Pallas kernels: 101 us -> 96.1 us  [shards(): pl.pallas_call(kernel, out_shape=jax.ShapeDtypeStruct((256, 96), jnp.bflo...]
where the time goes in v3:
time: 98.2 us; the launch traced here: 97.6 us
  Pallas kernels  96.1 us (98%)
  local copies, waits for them, and re-layouts  1.56 us (2%)
    pallas_call x1, Pallas kernels, shards(): pl.pallas_call(kernel, out_shape=jax.ShapeDtypeStruct((256, 96), jnp.bflo...  96.1 us

profile of v3, /device:TPU:1, one launch (start us, length us, event | category | flops | bytes accessed | tf_op | source)
XLA Modules:
  0.0 97.6 jit_solution(8656064508233837592)
XLA Ops:
  0.0 96.1 %shard_map.17 = bf16[256,96]{1,0:T(8,128)(2,1)} custom-call(bf16[16,4,384]{2,1,0:T(4,128)(2,1)} %bitcast.3), custom_call_target="tpu_custom_call" | custom-call | tf_op jit(solution)/shard_map/pallas_call | solution.py:372
  96.1 1.6 %copy.2 = bf16[256,96]{0,1:T(8,128)(2,1)} copy(bf16[256,96]{1,0:T(8,128)(2,1)} %shard_map.17) | data formatting | bytes 98304 | tf_op jit(solution)/shard_map/pallas_call | solution.py:372

commit v4 on v3

--- a/solution.py
+++ b/solution.py
@@ -21,6 +21,7 @@
 WIDE = 384
 STEPS = 16
 STRIDE = 3
+LEAVES = (14, 16)
 PARTS = 2
 PIECE = ROWS // PARTS
 
@@ -131,7 +132,7 @@
         px, py = peer(dx, dy)
         pl.semaphore_signal(barrier, inc=1, device_id=device(px, py, z, core), device_id_type=MESH)
     greeted = [(x, y, column(far), core) for far in REACH]
-    greeted.append((x, y, z, 1 - core))
+    greeted += [(x, y, column(far), 1 - core) for far in (1, 0, -1)]
     for target in greeted:
         pl.semaphore_signal(barrier, inc=1, device_id=device(*target), device_id_type=MESH)
     pl.semaphore_wait(barrier, 15 + len(greeted))
@@ -166,7 +167,7 @@
         return xg.at[pl.ds(start + PIECE * part_of, PIECE), :]
 
     def sem_at(far, sign):
-        return far if sign > 0 else STEPS + far
+        return far if sign > 0 or far == STEPS else STEPS + far
 
     def signs(far):
         return (1,) if far in (0, STEPS) else (1, -1)
@@ -174,7 +175,7 @@
     def hand_on(far, which, piece):
         for child in CHILDREN[far]:
             for sign in which:
-                if child == STEPS and sign < 0:
+                if child == STEPS and (sign > 0) != (piece < PARTS // 2):
                     continue
                 at = sem_at(child, sign)
                 sends.append(
@@ -186,6 +187,16 @@
                         device(x, y, column(sign * (child - far)), core),
                     )
                 )
+                if child in LEAVES:
+                    sends.append(
+                        push(
+                            slot(far, sign, True, piece),
+                            slot(child, sign, False, piece),
+                            twin_send.at[piece, at],
+                            twin_recv.at[piece, at],
+                            device(x, y, column(sign * (child - far)), 1 - core),
+                        )
+                    )
 
     def share(far):
         for sign in signs(far):
@@ -194,15 +205,20 @@
                 push(
                     slot(far, sign, True),
                     slot(far, sign, False),
-                    twin_send.at[at],
-                    twin_recv.at[at],
+                    twin_send.at[0, at],
+                    twin_recv.at[0, at],
                     twin,
                 )
             )
 
     def shared(far):
         for sign in signs(far):
-            await_bytes(slot(far, sign, False), twin_recv.at[sem_at(far, sign)])
+            at = sem_at(far, sign)
+            if far in LEAVES:
+                for piece in range(PARTS):
+                    await_bytes(slot(far, sign, False, piece), twin_recv.at[piece, at])
+            else:
+                await_bytes(slot(far, sign, False), twin_recv.at[0, at])
 
     tile = xg.at[pl.ds(last, ROWS), :]
 
@@ -264,7 +280,8 @@
             for sign in signs(far):
                 await_bytes(slot(far, sign, True, piece), ring_recv.at[piece, sem_at(far, sign)])
                 hand_on(far, (sign,), piece)
-        share(far)
+        if far not in LEAVES:
+            share(far)
         while groups and arrival(ORDER[groups[0]]) + 4.0 <= now:
             group = groups.pop(0)
             shared(ORDER[group])
@@ -388,8 +405,8 @@
             pltpu.SemaphoreType.DMA((2,)),
             pltpu.SemaphoreType.DMA((PARTS, 32)),
             pltpu.SemaphoreType.DMA((PARTS, 32)),
-            pltpu.SemaphoreType.DMA((32,)),
-            pltpu.SemaphoreType.DMA((32,)),
+            pltpu.SemaphoreType.DMA((PARTS, 32)),
+            pltpu.SemaphoreType.DMA((PARTS, 32)),
             pltpu.SemaphoreType.DMA((2, 4)),
             pltpu.SemaphoreType.DMA((2, 4)),
             pltpu.SemaphoreType.DMA((2, 4)),

time: 98.2 us -> 98.6 us (level)
  no operation moved by 1% of the time
where the time goes in v4:
time: 98.6 us; the launch traced here: 98.4 us
  Pallas kernels  96.8 us (98%)
  local copies, waits for them, and re-layouts  1.56 us (2%)
    pallas_call x1, Pallas kernels, shards(): pl.pallas_call(kernel, out_shape=jax.ShapeDtypeStruct((256, 96), jnp.bflo...  96.8 us

profile of v4, /device:TPU:1, one launch (start us, length us, event | category | flops | bytes accessed | tf_op | source)
XLA Modules:
  0.0 98.4 jit_solution(14699784082491347255)
XLA Ops:
  0.0 96.8 %shard_map.17 = bf16[256,96]{1,0:T(8,128)(2,1)} custom-call(bf16[16,4,384]{2,1,0:T(4,128)(2,1)} %bitcast.3), custom_call_target="tpu_custom_call" | custom-call | tf_op jit(solution)/shard_map/pallas_call | solution.py:389
  96.8 1.6 %copy.2 = bf16[256,96]{0,1:T(8,128)(2,1)} copy(bf16[256,96]{1,0:T(8,128)(2,1)} %shard_map.17) | data formatting | bytes 98304 | tf_op jit(solution)/shard_map/pallas_call | solution.py:389
